TPU v7x, 512 devices: a whole 4x4x16 slice. The times are simulated.
512 devices in a mesh: segment: 16 (over z_lo, x), dp: 8 (over y, core), mp: 4 (over z_hi).
Axes of the slice: x: 4, y: 4, z: 16 (z_hi: 4, z_lo: 4; z = z_hi * 4 + z_lo), core: 2. Of those that a mesh axis runs over, the one named last changes fastest.
Arguments:
- encoder_image_states: bfloat16 [8, 128, 8192], P('dp', 'segment'), may hold values from -6 to 6
- frozen_key_value: bfloat16 [16, 8192, 2, 1024], P('segment', 'dp', None, 'mp'), may hold values from -0.0625 to 0.0625
- adapter_down_weight: bfloat16 [16, 8192, 128], P('segment', 'mp'), may hold values from -0.0625 to 0.0625
- adapter_up_weight: bfloat16 [16, 2, 64, 1024], P('segment', None, None, 'mp'), may hold values from -0.75 to 0.75
- queries: bfloat16 [16, 8, 128, 8192], P('segment', 'dp', None, 'mp'), may hold values from -9 to 9
- cotangent: bfloat16 [16, 8, 128, 8192], P('segment', 'dp', None, 'mp'), may hold values from -1.5 to 1.5
- text_token_length: int32 [8], P('dp'), may hold values from 32 to 128
- image_tile_count: int32 [8], P('dp'), may hold values from 1 to 4
Outputs:
- grad_down: bfloat16 [16, 8192, 128], P('segment', 'mp')
- up_gradient: bfloat16 [16, 2, 64, 1024], P('segment', None, None, 'mp')
- grad_image: float32 [8, 128, 8192], P('dp', 'segment')
All inputs are finite; a program needn't handle non-finite values.
Results may differ from a plain program's by a relative error of at most 0.017.
The roundings to bfloat16 on the way count: a program that leaves them out, or rounds other values in their place, can miss the bound.
Values may be sent and summed in bfloat16 or wider, within the bound.
No kernel may reach another device: no remote copies, remote signals or barrier semaphores. Data moves between devices by JAX's collectives and lax.ppermute only.
A program may use at most 64 MiB of HBM per device.

v0:
```python
import jax
import jax.numpy as jnp
from jax import lax
from jax.sharding import PartitionSpec as P

HD = 128
TILES = 4
adapter_scale = 2.0
contract_rows = (((0,), (0,)), ((), ()))
contracted_columns = (((1,), (1,)), ((), ()))


def body(
    encoder_image_states,
    frozen_key_value,
    adapter_down_weight,
    adapter_up_weight,
    queries,
    cotangent,
    text_token_length,
    image_tile_count,
):
    samples = encoder_image_states.shape[0]
    model_width = encoder_image_states.shape[2]
    whole_img = lax.all_gather(encoder_image_states, "segment", axis=1, tiled=True)
    image_rows = whole_img.shape[1]
    flat_rows = samples * image_rows
    flat_img = whole_img.reshape(flat_rows, model_width)
    fourth_part = adapter_down_weight.shape[1]
    parallel_index = lax.axis_index("mp")
    image_fourth = lax.dynamic_slice_in_dim(flat_img, parallel_index * fourth_part, fourth_part, 1)
    lowrank_state = adapter_up_weight.shape[2]
    key_value_columns = adapter_up_weight.shape[3]
    lowrank_projection = lax.psum(
        jnp.dot(image_fourth, adapter_down_weight[0], preferred_element_type=jnp.float32), "mp"
    ).astype(jnp.bfloat16)
    adapted_weight = jnp.concatenate(
        [
            jnp.dot(
                lowrank_projection[:, :lowrank_state],
                adapter_up_weight[0, 0],
                preferred_element_type=jnp.float32,
            ),
            jnp.dot(
                lowrank_projection[:, lowrank_state:],
                adapter_up_weight[0, 1],
                preferred_element_type=jnp.float32,
            ),
        ],
        axis=1,
    )
    local_weight = frozen_key_value[0]
    full_weight = lax.all_gather(local_weight, "dp", axis=0, tiled=True).reshape(
        model_width, 2 * key_value_columns
    )
    frozen_output = jnp.dot(flat_img, full_weight, preferred_element_type=jnp.float32)
    key_value_pair = (frozen_output + adapter_scale * adapted_weight).astype(jnp.bfloat16)
    local_heads = queries.shape[3] // HD
    local_kv = key_value_columns // HD
    group_size = local_heads // local_kv
    text_rows = queries.shape[2]
    query_rows = queries[0].reshape(samples, text_rows, local_kv, group_size, HD)
    cot_rows = cotangent[0].reshape(samples, text_rows, local_kv, group_size, HD)
    key_rows = key_value_pair[:, :key_value_columns].reshape(samples, image_rows, local_kv, HD)
    value_rows = key_value_pair[:, key_value_columns:].reshape(samples, image_rows, local_kv, HD)
    key_mask = jnp.arange(image_rows, dtype=jnp.int32)[None, :] < image_tile_count[:, None] * (
        image_rows // TILES
    )
    row_mask = (
        jnp.arange(text_rows, dtype=jnp.int32)[None, :] < text_token_length[:, None]
    ).astype(jnp.float32)
    scores = jnp.einsum(
        "btgrd,bjgd->bgrtj", query_rows, key_rows, preferred_element_type=jnp.float32
    ) * HD ** (-0.5)
    masked = jnp.where(key_mask[:, None, None, None, :], scores, -1e30)
    row_top = jnp.max(masked, axis=-1, keepdims=True)
    shifted = jnp.exp(masked - row_top)
    attention = shifted / jnp.sum(shifted, axis=-1, keepdims=True)
    row_gate = row_mask[:, None, None, :, None]
    kept = attention.astype(jnp.bfloat16) * row_gate.astype(jnp.bfloat16)
    dweights = jnp.einsum(
        "btgrd,bjgd->bgrtj", cot_rows, value_rows, preferred_element_type=jnp.float32
    )
    row_delta = jnp.sum(attention * dweights, axis=-1, keepdims=True)
    dscore = (attention * (dweights - row_delta) * row_gate * HD ** (-0.5)).astype(jnp.bfloat16)
    key_grad = jnp.einsum(
        "bgrtj,btgrd->bjgd", dscore, query_rows, preferred_element_type=jnp.float32
    )
    value_grad = jnp.einsum("bgrtj,btgrd->bjgd", kept, cot_rows, preferred_element_type=jnp.float32)
    kv_grad = jnp.concatenate(
        [
            key_grad.reshape(flat_rows, key_value_columns),
            value_grad.reshape(flat_rows, key_value_columns),
        ],
        axis=1,
    ).astype(jnp.bfloat16)
    backward_piece = adapter_scale * jnp.concatenate(
        [
            lax.dot_general(
                kv_grad[:, :key_value_columns],
                adapter_up_weight[0, 0],
                contracted_columns,
                preferred_element_type=jnp.float32,
            ),
            lax.dot_general(
                kv_grad[:, key_value_columns:],
                adapter_up_weight[0, 1],
                contracted_columns,
                preferred_element_type=jnp.float32,
            ),
        ],
        axis=1,
    )
    backward_lowrank = lax.psum(backward_piece, "mp").astype(jnp.bfloat16)
    up_gradient = adapter_scale * jnp.stack(
        [
            lax.dot_general(
                lowrank_projection[:, :lowrank_state],
                kv_grad[:, :key_value_columns],
                contract_rows,
                preferred_element_type=jnp.float32,
            ),
            lax.dot_general(
                lowrank_projection[:, lowrank_state:],
                kv_grad[:, key_value_columns:],
                contract_rows,
                preferred_element_type=jnp.float32,
            ),
        ]
    )
    grad_down = lax.dot_general(
        image_fourth, backward_lowrank, contract_rows, preferred_element_type=jnp.float32
    )
    down_sum, up_sum = lax.psum((grad_down, up_gradient), "dp")
    image_gradient_total = lax.dot_general(
        kv_grad, full_weight, contracted_columns, preferred_element_type=jnp.float32
    )
    adapter_portion = lax.dot_general(
        backward_lowrank,
        adapter_down_weight[0],
        contracted_columns,
        preferred_element_type=jnp.float32,
    )
    current_layer = lax.dynamic_slice_in_dim(
        image_gradient_total, parallel_index * fourth_part, fourth_part, 1
    )
    image_gradient_total = lax.dynamic_update_slice_in_dim(
        image_gradient_total, current_layer + adapter_portion, parallel_index * fourth_part, 1
    )
    image_gradient_total = image_gradient_total.reshape(samples, image_rows, model_width)
    shared_sum = lax.psum_scatter(image_gradient_total, "segment", scatter_dimension=1, tiled=True)
    result = lax.psum(shared_sum, "mp")
    return (down_sum.astype(jnp.bfloat16)[None], up_sum.astype(jnp.bfloat16)[None], result)


def solution(mesh):
    in_specs = (
        P("dp", "segment", None),
        P("segment", "dp", None, "mp"),
        P("segment", "mp", None),
        P("segment", None, None, "mp"),
        P("segment", "dp", None, "mp"),
        P("segment", "dp", None, "mp"),
        P("dp"),
        P("dp"),
    )
    out_specs = (P("segment", "mp", None), P("segment", None, None, "mp"), P("dp", "segment", None))
    return jax.shard_map(body, mesh=mesh, in_specs=in_specs, out_specs=out_specs, check_vma=False)
```

profile of v0, /device:TPU:2, one launch (start us, length us, event | category | flops | bytes accessed | tf_op | source)
XLA Modules:
  0.0 390.2 jit_solution(4577795114373816345)
XLA Ops:
  7.2 0.7 all-gather.4.cloned.1.call-update
  8.0 0.7 all-gather.6.cloned.1.call-update
  10.0 1.3 copy.38
  11.3 2.0 copy.39
  13.4 88.8 %all-gather.4.cloned.1.call-done = bf16[1,128,8192]{2,1,0:T(8,128)(2,1)} async-done(((bf16[1,8,8192]{2,1,0:T(8,128)(2,1)}), bf16[1,128,8192]{2,1,0:T(8,128)(2,1)}) %all-gather.4.cloned.1.call-update) | async-done | bytes 2097168 | tf_op jit(solution)/shard_map/all_gather | solution.py:25
  102.2 1.3 fusion.21
  103.6 25.9 %psum.35 = bf16[128,128]{1,0:T(8,128)(2,1)S(1)} all-reduce(f32[128,128]{1,0:T(8,128)S(1)} %fusion.21), channel_id=1, replica_groups=mesh['segment'=16,'dp'=8,'mp'=4] {'mp'}, use_global_device_ids=true, to_apply=%region_0.0 | all-reduce | flops 16384 | bytes 98304 | tf_op jit(solution)/shard_map/psum | solution.py:34
  129.8 30.6 %all-gather.6.cloned.1.call-done = bf16[1,8192,2,256]{3,2,0,1:T(2,128)(2,1)} async-done(((bf16[1,1024,2,256]{3,2,0,1:T(2,128)(2,1)}), bf16[1,8192,2,256]{3,2,0,1:T(2,128)(2,1)}) %all-gather.6.cloned.1.call-update) | async-done | bytes 8388624 | tf_op jit(solution)/shard_map/all_gather | solution.py:53
  160.5 8.2 %copy.40 = bf16[1024,8,2,256]{3,1,2,0:T(8,128)(2,1)} copy(bf16[1024,8,2,256]{3,2,1,0:T(2,128)(2,1)} %bitcast.113) | data formatting | bytes 16777216
  168.6 4.6 %fusion.10 = bf16[128,512]{1,0:T(8,128)(2,1)S(1)} fusion(bf16[8192,512]{1,0:T(8,128)(2,1)} %bitcast.108, bf16[1,128,8192]{2,1,0:T(8,128)(2,1)S(1)} %copy-done.1, f32[128,256]{1,0:T(8,128)S(1)} %fusion.42, f32[128,256]{1,0:T(8,128)S(1)} %fusion.46), kind=kOutput, calls=%fused_computation.11 | convolution fusion | flops 1074003968 | bytes 10878976 | tf_op jit(solution)/shard_map/dot_general | solution.py:56
  173.3 0.3 fusion.66
  173.8 1.6 fusion.14
  175.6 0.3 multiply_reduce_fusion
  175.9 0.5 fusion.13
  176.4 1.5 slice-done.1
  177.9 4.8 %fusion.34 = f32[128,8192]{1,0:T(8,128)} fusion(bf16[8192,512]{1,0:T(8,128)(2,1)S(1)} %bitcast.111, bf16[128,256]{0,1:T(8,128)(2,1)S(1)} %bitcast.118, bf16[128,256]{0,1:T(8,128)(2,1)S(1)} %bitcast.120), kind=kOutput, calls=%fused_computation.42 | convolution fusion | flops 1074003968 | bytes 12713984 | tf_op jit(solution)/shard_map/dot_general | solution.py:135
  182.8 26.9 %psum.36 = bf16[128,128]{0,1:T(8,128)(2,1)S(1)} all-reduce(f32[128,128]{0,1:T(8,128)S(1)} %maximum_multiply_fusion.2), channel_id=1, replica_groups=mesh['segment'=16,'dp'=8,'mp'=4] {'mp'}, use_global_device_ids=true, to_apply=%region_4.5 | all-reduce | flops 16384 | bytes 98304 | tf_op jit(solution)/shard_map/psum | solution.py:114
  209.8 4.6 %copy.51 = f32[1,128,8192]{2,1,0:T(8,128)} copy(f32[1,128,8192]{2,1,0:T(8,128)} %bitcast.112) | data formatting | bytes 8388608
  214.3 2.5 fusion.1
  216.9 1.3 fusion.23
  218.7 89.1 %reduce-scatter.2.cloned.1.call-done = f32[1,8,8192]{2,1,0:T(8,128)} async-done(((f32[1,128,8192]{2,1,0:T(8,128)}), f32[1,8,8192]{2,1,0:T(8,128)}) %reduce-scatter.2.cloned.1.call-update) | async-done | bytes 262160 | tf_op jit(solution)/shard_map/reduce_scatter | solution.py:151
  307.7 52.3 %all-reduce.5 = (bf16[2048,128]{1,0:T(8,128)(2,1)}, bf16[2,64,256]{2,1,0:T(8,128)(2,1)}) all-reduce(f32[2048,128]{1,0:T(8,128)} %fusion.23, f32[2,64,256]{2,1,0:T(8,128)S(1)} %maximum_multiply_fusion.1), channel_id=1, replica_groups=mesh['segment'=16,'dp'=8,'mp'=4] {'dp'}, use_global_device_ids=true, to_apply=%region_5.6 | all-reduce | flops 294912 | bytes 1769472 | tf_op jit(solution)/shard_map/psum | solution.py:134
  360.0 22.0 %all-reduce.4.cloned.1.call-done = f32[1,8,8192]{2,1,0:T(8,128)} async-done(((f32[1,8,8192]{2,1,0:T(8,128)}), f32[1,8,8192]{2,1,0:T(8,128)}) %all-reduce.4.cloned.1.call-update) | async-done | bytes 262160 | tf_op jit(solution)/shard_map/psum | solution.py:152
  382.0 1.7 copy.57
  (32 shorter events, 1.5 us)
Async XLA Ops:
  7.2 95.1 %copy-start = (bf16[1,2048,128]{2,1,0:T(8,128)(2,1)S(1)}, bf16[1,2048,128]{2,1,0:T(8,128)(2,1)}, u32[]{:S(2)}) copy-start(bf16[1,2048,128]{2,1,0:T(8,128)(2,1)} %param.10) | copy-start | bytes 1572868
  7.2 122.3 %copy-start.3 = (bf16[1,2,64,256]{3,2,1,0:T(8,128)(2,1)S(1)}, bf16[1,2,64,256]{3,2,1,0:T(8,128)(2,1)}, u32[]{:S(2)}) copy-start(bf16[1,2,64,256]{3,2,1,0:T(8,128)(2,1)} %param.11) | copy-start | bytes 196612
  7.2 95.0 %all-gather.4.cloned.1.call-start = ((), (), s32[]{:S(2)}) async-start(), calls=%async_computation.1 | async-start | bytes 2228224 | tf_op jit(solution)/shard_map/all_gather | solution.py:25
  7.9 152.5 %all-gather.6.cloned.1.call-start = ((), (), s32[]{:S(2)}) async-start(), calls=%async_computation.4 | async-start | bytes 9437184 | tf_op jit(solution)/shard_map/all_gather | solution.py:53
  8.7 299.0 %reduce-scatter.2.cloned.1.call-start = ((), (), s32[]{:S(2)}) async-start(), calls=%async_computation.2 | async-start | bytes 4456448 | tf_op jit(solution)/shard_map/reduce_scatter | solution.py:151
  160.5 8.2 %copy-start.1 = (bf16[1,128,8192]{2,1,0:T(8,128)(2,1)S(1)}, bf16[1,128,8192]{2,1,0:T(8,128)(2,1)}, u32[]{:S(2)}) copy-start(bf16[1,128,8192]{2,1,0:T(8,128)(2,1)} %all-gather.4.cloned.1.call-done) | copy-start | bytes 6291460
  173.3 2.2 copy-start.2
  173.8 2.6 slice-start
  175.6 2.4 slice-start.1
  216.8 165.2 %all-reduce.4.cloned.1.call-start = ((), (), s32[]{:S(2)}) async-start(), calls=%async_computation.3 | async-start | bytes 524288 | tf_op jit(solution)/shard_map/psum | solution.py:152
Sparse Core Ops, SparseCore 0:
  10.1 92.1 all-gather.3
  104.4 56.0 all-gather.5
  217.0 90.7 reduce-scatter.1
  310.5 71.4 all-reduce.3
where the time goes:
time: 391 us; the launch traced here: 390 us
  waiting for transfers between devices  232 us (59%)
  blocking collectives  105 us (27%)
  local copies, waits for them, and re-layouts  19.3 us (5%)
  matrix products  18.3 us (5%)
  between operations  15.2 us (4%)
    reduce_scatter x1, waiting for transfers between devices, body(): lax.psum_scatter(image_gradient_total, 'segment', scatter_dimension=1, ti...  89.1 us
    all_gather x1, waiting for transfers between devices, body(): lax.all_gather(encoder_image_states, 'segment', axis=1, tiled=True)  88.8 us
    psum x1, blocking collectives, body(): down_sum, up_sum = lax.psum((grad_down, up_gradient), 'dp')  52.3 us
    all_gather x1, waiting for transfers between devices, body(): lax.all_gather(local_weight, 'dp', axis=0, tiled=True)  30.6 us
    psum x1, blocking collectives, body(): backward_lowrank = lax.psum(backward_piece, 'mp').astype(jnp.bfloat16)  26.9 us
    psum x1, blocking collectives, body(): lax.psum(jnp.dot(image_fourth, adapter_down_weight[0], preferred_element_...  25.9 us
    psum x1, waiting for transfers between devices, body(): result = lax.psum(shared_sum, 'mp')  22 us
    unnamed x15, local copies, waits for them, and re-layouts  15.9 us
  transfers between devices with their start and end apart: 4, of which 4 were waited for; matrix products, arithmetic and copies ran while one was open for 2% of the time, Pallas kernels for 0%

commit v1 on v0

--- a/solution.py
+++ b/solution.py
@@ -22,7 +22,12 @@
 ):
     samples = encoder_image_states.shape[0]
     model_width = encoder_image_states.shape[2]
-    whole_img = lax.all_gather(encoder_image_states, "segment", axis=1, tiled=True)
+    whole_img = jnp.concatenate(
+        jax.lax.all_to_all(
+            jnp.stack([encoder_image_states] * jax.lax.axis_size("segment"), 0), "segment", 0, 0
+        ),
+        1,
+    )
     image_rows = whole_img.shape[1]
     flat_rows = samples * image_rows
     flat_img = whole_img.reshape(flat_rows, model_width)

time: 391 us -> 324 us (0.83)
  waiting for transfers between devices: 232 us -> 155 us
  starting transfers between devices: 0.16 us -> 9.63 us
    all_gather x1 -> x0, waiting for transfers between devices: 88.8 us -> none  [body(): lax.all_gather(encoder_image_states, 'segment', axis=1, tiled=True)]
    all_to_all x0 -> x1, waiting for transfers between devices: none -> 36.1 us  [body(): jax.lax.all_to_all(jnp.stack([encoder_image_states] * jax.lax.axis_size('...]
    all_gather x1, waiting for transfers between devices: 30.6 us -> 0.02 us  [body(): lax.all_gather(local_weight, 'dp', axis=0, tiled=True)]
    all_to_all x0 -> x1, starting transfers between devices: none -> 9.52 us  [body(): jax.lax.all_to_all(jnp.stack([encoder_image_states] * jax.lax.axis_size('...]
    reduce_scatter x1, waiting for transfers between devices: 89.1 us -> 96.1 us  [body(): lax.psum_scatter(image_gradient_total, 'segment', scatter_dimension=1, ti...]
    unnamed x15 -> x13, local copies, waits for them, and re-layouts: 15.9 us -> 15.7 us
  transfers between devices with their start and end apart: 4 -> 4, of which waited for: 4 -> 3; matrix products, arithmetic and copies ran while one was open for 2% -> 3% of each run, Pallas kernels for 0% -> 0%
where the time goes in v1:
time: 324 us; the launch traced here: 323 us
  waiting for transfers between devices  155 us (48%)
  blocking collectives  104 us (32%)
  local copies, waits for them, and re-layouts  21.6 us (7%)
  matrix products  17.4 us (5%)
  between operations  15.2 us (5%)
  starting transfers between devices  9.63 us (3%)
    reduce_scatter x1, waiting for transfers between devices, body(): lax.psum_scatter(image_gradient_total, 'segment', scatter_dimension=1, ti...  96.1 us
    psum x1, blocking collectives, body(): down_sum, up_sum = lax.psum((grad_down, up_gradient), 'dp')  52.3 us
    all_to_all x1, waiting for transfers between devices, body(): jax.lax.all_to_all(jnp.stack([encoder_image_states] * jax.lax.axis_size('...  36.1 us
    psum x1, blocking collectives, body(): lax.psum(jnp.dot(image_fourth, adapter_down_weight[0], preferred_element_...  28.4 us
    psum x1, blocking collectives, body(): backward_lowrank = lax.psum(backward_piece, 'mp').astype(jnp.bfloat16)  23.7 us
    psum x1, waiting for transfers between devices, body(): result = lax.psum(shared_sum, 'mp')  22 us
    unnamed x13, local copies, waits for them, and re-layouts  15.7 us
    all_to_all x1, starting transfers between devices, body(): jax.lax.all_to_all(jnp.stack([encoder_image_states] * jax.lax.axis_size('...  9.52 us
  transfers between devices with their start and end apart: 4, of which 3 were waited for; matrix products, arithmetic and copies ran while one was open for 3% of the time, Pallas kernels for 0%

profile of v1, /device:TPU:2, one launch (start us, length us, event | category | flops | bytes accessed | tf_op | source)
XLA Modules:
  0.0 323.4 jit_solution(5856999373383504148)
XLA Ops:
  7.2 0.7 all-gather.3.cloned.1.call-update
  7.9 2.5 stack.8
  10.4 9.5 %all-to-all-start = ((bf16[16,1,8,8192]{3,2,1,0:T(8,128)(2,1)}), bf16[16,1,8,8192]{3,2,1,0:T(8,128)(2,1)S(1)}, u32[]{:S(2)}, u32[]{:S(2)}) async-start(bf16[16,1,8,8192]{3,2,1,0:T(8,128)(2,1)} %stack.8), calls=%async_computation | async-start | bytes 4194304 | tf_op jit(solution)/shard_map/all_to_all | solution.py:26
  21.3 1.3 copy.38
  22.6 2.0 copy.39
  24.7 36.1 %all-to-all-done = bf16[16,1,8,8192]{3,2,1,0:T(8,128)(2,1)S(1)} async-done(((bf16[16,1,8,8192]{3,2,1,0:T(8,128)(2,1)}), bf16[16,1,8,8192]{3,2,1,0:T(8,128)(2,1)S(1)}, u32[]{:S(2)}, u32[]{:S(2)}) %all-to-all-start) | async-done | bytes 2097184 | tf_op jit(solution)/shard_map/all_to_all | solution.py:26
  60.7 0.3 fusion.14
  61.0 28.4 %psum.35 = bf16[128,128]{1,0:T(8,128)(2,1)S(1)} all-reduce(f32[128,128]{1,0:T(8,128)S(1)} %fusion.14), channel_id=1, replica_groups=mesh['segment'=16,'dp'=8,'mp'=4] {'mp'}, use_global_device_ids=true, to_apply=%region_0.0 | all-reduce | flops 16384 | bytes 98304 | tf_op jit(solution)/shard_map/psum | solution.py:39
  89.9 8.0 %copy.40 = bf16[1024,8,2,256]{3,1,2,0:T(8,128)(2,1)} copy(bf16[1024,8,2,256]{3,2,1,0:T(2,128)(2,1)} %bitcast.107) | data formatting | bytes 16777216
  97.9 4.6 %fusion.5 = bf16[128,512]{1,0:T(8,128)(2,1)S(1)} fusion(bf16[8192,512]{1,0:T(8,128)(2,1)} %bitcast.100, f32[128,256]{1,0:T(8,128)S(1)} %fusion.33, f32[128,256]{1,0:T(8,128)S(1)} %fusion.37, bf16[16,1,8,8192]{3,2,1,0:T(8,128)(2,1)S(1)} %all-to-all-done), kind=kOutput, calls=%fused_computation.9 | convolution fusion | flops 1074003968 | bytes 10878976 | tf_op jit(solution)/shard_map/dot_general | solution.py:61
  102.6 0.3 fusion.58
  103.1 1.6 fusion.7
  104.8 0.3 multiply_reduce_fusion
  105.2 0.5 fusion.6
  105.7 1.4 slice-done.1
  107.2 4.8 %fusion.25 = f32[128,8192]{1,0:T(8,128)} fusion(bf16[8192,512]{1,0:T(8,128)(2,1)S(1)} %bitcast.103, bf16[128,256]{0,1:T(8,128)(2,1)S(1)} %bitcast.112, bf16[128,256]{0,1:T(8,128)(2,1)S(1)} %bitcast.114), kind=kOutput, calls=%fused_computation.38 | convolution fusion | flops 1074003968 | bytes 12713984 | tf_op jit(solution)/shard_map/dot_general | solution.py:140
  112.1 23.7 %psum.36 = bf16[128,128]{0,1:T(8,128)(2,1)S(1)} all-reduce(f32[128,128]{0,1:T(8,128)S(1)} %maximum_multiply_fusion.2), channel_id=1, replica_groups=mesh['segment'=16,'dp'=8,'mp'=4] {'mp'}, use_global_device_ids=true, to_apply=%region_4.5 | all-reduce | flops 16384 | bytes 98304 | tf_op jit(solution)/shard_map/psum | solution.py:119
  135.8 4.6 %copy.51 = f32[1,128,8192]{2,1,0:T(8,128)} copy(f32[1,128,8192]{2,1,0:T(8,128)} %bitcast.106) | data formatting | bytes 8388608
  140.3 2.6 fusion.1
  143.0 1.3 fusion.21
  144.8 96.1 %reduce-scatter.2.cloned.1.call-done = f32[1,8,8192]{2,1,0:T(8,128)} async-done(((f32[1,128,8192]{2,1,0:T(8,128)}), f32[1,8,8192]{2,1,0:T(8,128)}) %reduce-scatter.2.cloned.1.call-update) | async-done | bytes 262160 | tf_op jit(solution)/shard_map/reduce_scatter | solution.py:156
  240.9 52.3 %all-reduce.5 = (bf16[2048,128]{1,0:T(8,128)(2,1)}, bf16[2,64,256]{2,1,0:T(8,128)(2,1)}) all-reduce(f32[2048,128]{1,0:T(8,128)} %fusion.21, f32[2,64,256]{2,1,0:T(8,128)S(1)} %maximum_multiply_fusion.1), channel_id=1, replica_groups=mesh['segment'=16,'dp'=8,'mp'=4] {'dp'}, use_global_device_ids=true, to_apply=%region_5.6 | all-reduce | flops 294912 | bytes 1769472 | tf_op jit(solution)/shard_map/psum | solution.py:139
  293.2 22.0 %all-reduce.4.cloned.1.call-done = f32[1,8,8192]{2,1,0:T(8,128)} async-done(((f32[1,8,8192]{2,1,0:T(8,128)}), f32[1,8,8192]{2,1,0:T(8,128)}) %all-reduce.4.cloned.1.call-update) | async-done | bytes 262160 | tf_op jit(solution)/shard_map/psum | solution.py:157
  315.2 1.7 copy.57
  (30 shorter events, 1.5 us)
Async XLA Ops:
  7.2 53.6 %copy-start = (bf16[1,2048,128]{2,1,0:T(8,128)(2,1)S(1)}, bf16[1,2048,128]{2,1,0:T(8,128)(2,1)}, u32[]{:S(2)}) copy-start(bf16[1,2048,128]{2,1,0:T(8,128)(2,1)} %param.10) | copy-start | bytes 1572868
  7.2 82.7 %all-gather.3.cloned.1.call-start = ((), (), s32[]{:S(2)}) async-start(), calls=%async_computation.4 | async-start | bytes 9437184 | tf_op jit(solution)/shard_map/all_gather | solution.py:58
  10.4 79.1 %copy-start.2 = (bf16[1,2,64,256]{3,2,1,0:T(8,128)(2,1)S(1)}, bf16[1,2,64,256]{3,2,1,0:T(8,128)(2,1)}, u32[]{:S(2)}) copy-start(bf16[1,2,64,256]{3,2,1,0:T(8,128)(2,1)} %param.11) | copy-start | bytes 196612
  10.4 50.3 %all-to-all-start = ((bf16[16,1,8,8192]{3,2,1,0:T(8,128)(2,1)}), bf16[16,1,8,8192]{3,2,1,0:T(8,128)(2,1)S(1)}, u32[]{:S(2)}, u32[]{:S(2)}) async-start(bf16[16,1,8,8192]{3,2,1,0:T(8,128)(2,1)} %stack.8), calls=%async_computation | async-start | bytes 4194304 | tf_op jit(solution)/shard_map/all_to_all | solution.py:26
  19.9 220.9 %reduce-scatter.2.cloned.1.call-start = ((), (), s32[]{:S(2)}) async-start(), calls=%async_computation.2 | async-start | bytes 4456448 | tf_op jit(solution)/shard_map/reduce_scatter | solution.py:156
  102.6 2.2 copy-start.1
  103.1 2.7 slice-start
  104.8 2.4 slice-start.1
  142.9 172.3 %all-reduce.4.cloned.1.call-start = ((), (), s32[]{:S(2)}) async-start(), calls=%async_computation.3 | async-start | bytes 524288 | tf_op jit(solution)/shard_map/psum | solution.py:157
Sparse Core Ops, SparseCore 0:
  10.1 61.7 all-gather.2
  143.0 97.7 reduce-scatter.1
  243.8 71.3 all-reduce.3
